TPU v7x, 128 devices: a whole 4x4x4 slice. The times are simulated.
128 devices in a mesh: section: 16 (over y_lo, z, core), dp: 8 (over x, y_hi).
Axes of the slice: x: 4, y: 4 (y_hi: 2, y_lo: 2; y = y_hi * 2 + y_lo), z: 4, core: 2. Of those that a mesh axis runs over, the one named last changes fastest.
Arguments:
- first_acts: bfloat16 [16, 1024, 8192], P('section', 'dp'), may hold values from -6 to 6
- first_grads: bfloat16 [16, 1024, 8192], P('section', 'dp'), may hold values from -6 to 6
- last_acts: bfloat16 [16, 1024, 8192], P('section', 'dp'), may hold values from -6 to 6
- last_grads: bfloat16 [16, 1024, 8192], P('section', 'dp'), may hold values from -6 to 6
- doc_lengths: int32 [8, 16], P('dp'), may hold values from 1 to 32, 128 in all within a row
- block_owner: int32 [16], replicated, may hold values from 0 to 7, as said below
Outputs:
- act_factor: float32 [16, 8, 4, 512, 512], P('section', 'dp')
- grad_factor: float32 [16, 8, 4, 512, 512], P('section', 'dp')
- act_cross: float32 [16, 8, 4, 512, 512], P('section', 'dp')
- grad_cross: float32 [16, 8, 4, 512, 512], P('section', 'dp')
Inputs may be any that keep to these rules, and one draw needn't show every extreme that they name: `doc_lengths`: documents fill their group's 128 rows exactly and the longest is exactly 32 rows. `block_owner`: one owner holds exactly 4 blocks, one holds none, every other holds exactly 2; which ones is drawn, except that the first and the last group always own blocks.
All inputs are finite; a program needn't handle non-finite values.
Results may differ from a plain program's by a relative error of at most 0.0037.
Values may be sent and summed in bfloat16 or wider, within the bound.
No kernel may reach another device: no remote copies, remote signals or barrier semaphores. Data moves between devices by JAX's collectives and lax.ppermute only.
A program may use at most 320 MiB of HBM per device.

v0:
```python
import jax
import jax.numpy as jnp
from jax import lax
from jax.sharding import PartitionSpec as P


def shifted(block, axis, distance):
    devices = range(lax.axis_size(axis))
    route = [(i - distance, i) for i in devices if i - distance in devices]
    return lax.ppermute(block, axis, route)


def row_scale(doc_lengths, row_count, docs_all):
    doc_sizes = doc_lengths.astype(jnp.float32)
    doc_end = jnp.cumsum(doc_lengths)
    starts = doc_end - doc_lengths
    places = jnp.arange(row_count, dtype=jnp.int32)
    inside = (places[:, None] >= starts[None, :]) & (places[:, None] < doc_end[None, :])
    inverse = jnp.sum(jnp.where(inside, 1.0 / doc_sizes[None, :], jnp.float32(0.0)), axis=1)
    return jnp.sqrt(inverse / docs_all)


def slot_table(block_owner, groups, slot_count):
    blocks = block_owner.shape[0]
    position = jnp.arange(blocks, dtype=jnp.int32)
    same_owner = block_owner[:, None] == block_owner[None, :]
    earlier = position[None, :] < position[:, None]
    slot_index = jnp.sum(jnp.where(same_owner & earlier, 1, 0), axis=1).astype(jnp.int32)
    target = block_owner * slot_count + slot_index
    wanted = jnp.arange(groups * slot_count, dtype=jnp.int32)
    return jnp.where(wanted[:, None] == target[None, :], 1.0, 0.0).astype(jnp.bfloat16)


def into_slots(matrix, selector, groups, slot_count):
    row_count, widths = matrix.shape
    blocks = selector.shape[1]
    block_width = widths // blocks
    blocked = matrix.reshape(row_count, blocks, block_width)
    placed = jnp.einsum("cb,rbf->crf", selector, blocked, preferred_element_type=jnp.float32)
    return placed.astype(jnp.bfloat16).reshape(groups, slot_count, row_count, block_width)


def owner_gram(former, latter):
    return jnp.einsum("gkrf,gkrh->kfh", former, latter, preferred_element_type=jnp.float32)


def on_device(first_acts, first_grads, last_acts, last_grads, doc_lengths, block_owner):
    row_count = first_acts.shape[1]
    groups = lax.axis_size("dp")
    blocks = block_owner.shape[0]
    slot_count = 2 * blocks // groups
    row_weight = row_scale(doc_lengths[0], row_count, doc_lengths.shape[1] * groups)[:, None]

    def weighted(matrix):
        return (matrix[0].astype(jnp.float32) * row_weight).astype(jnp.bfloat16)

    own_acts = weighted(first_acts)
    own_grads = weighted(first_grads)
    tail_acts = weighted(last_acts)
    tail_grads = weighted(last_grads)
    selector = slot_table(block_owner, groups, slot_count)
    acts_in = lax.all_to_all(
        into_slots(own_acts, selector, groups, slot_count),
        "dp",
        split_axis=0,
        concat_axis=0,
        tiled=True,
    )
    grads_in = lax.all_to_all(
        into_slots(own_grads, selector, groups, slot_count),
        "dp",
        split_axis=0,
        concat_axis=0,
        tiled=True,
    )
    tail_in = lax.all_to_all(
        into_slots(tail_acts, selector, groups, slot_count),
        "dp",
        split_axis=0,
        concat_axis=0,
        tiled=True,
    )
    tail_grad_in = lax.all_to_all(
        into_slots(tail_grads, selector, groups, slot_count),
        "dp",
        split_axis=0,
        concat_axis=0,
        tiled=True,
    )
    prev_in, prev_grad_in = shifted((tail_in, tail_grad_in), "section", 1)
    first = owner_gram(acts_in, acts_in)
    second = owner_gram(grads_in, grads_in)
    third = owner_gram(prev_in, acts_in)
    fourth = owner_gram(prev_grad_in, grads_in)
    results = (first[None, None], second[None, None], third[None, None], fourth[None, None])
    return results


def solution(mesh):
    placed = (
        P("section", "dp", None),
        P("section", "dp", None),
        P("section", "dp", None),
        P("section", "dp", None),
        P("dp", None),
        P(),
    )
    return jax.shard_map(
        on_device,
        mesh=mesh,
        in_specs=placed,
        out_specs=(
            P("section", "dp", None, None, None),
            P("section", "dp", None, None, None),
            P("section", "dp", None, None, None),
            P("section", "dp", None, None, None),
        ),
        check_vma=False,
    )
```

profile of v0, /device:TPU:30, one launch (start us, length us, event | category | flops | bytes accessed | tf_op | source)
XLA Modules:
  0.0 364.1 jit_solution(6042393307211551714)
XLA Ops:
  9.2 5.4 %fusion = (bf16[128,16,512]{2,1,0:T(8,128)(2,1)}, bf16[128,16,512]{2,1,0:T(8,128)(2,1)S(1)}, bf16[128,16,512]{2,1,0:T(8,128)(2,1)}, bf16[128,16,512]{2,1,0:T(8,128)(2,1)S(1)}) fusion(f32[16,8,16,512]{3,2,1,0:T(8,128)S(1)} %copy.59, f32[128]{0:T(128)S(1)} %multiply_sqrt_fusion, f32[16,8,16,512]{3,2,1,0:T(8,128)S(1)} %copy.57, f32[16,8,16,512]{3,2,1,0:T(8,128)S(1)} %copy.58, ...), kind=kLoop, calls=%fused_computation.1 | loop fusion | flops 8388608 | bytes 25166336 | tf_op jit(solution)/shard_map/convert_element_type | solution.py:55
  15.9 4.4 %copy.53 = bf16[32,128,512]{2,1,0:T(8,128)(2,1)} copy(bf16[32,128,512]{2,0,1:T(8,128)(2,1)S(1)} %convolution_convert_fusion.2) | data formatting | bytes 8388608 | tf_op jit(solution)/shard_map/reshape | solution.py:40
  20.3 7.2 %all-to-all-start.1 = ((bf16[8,4,128,512]{3,2,1,0:T(8,128)(2,1)}), bf16[8,4,128,512]{3,2,1,0:T(8,128)(2,1)}, u32[]{:S(2)}, u32[]{:S(2)}) async-start(bf16[8,4,128,512]{3,2,1,0:T(8,128)(2,1)} %bitcast.78), calls=%async_computation.1 | async-start | bytes 8388608 | tf_op jit(solution)/shard_map/all_to_all | solution.py:69
  27.5 4.9 %convolution_convert_fusion = bf16[32,128,512]{2,0,1:T(8,128)(2,1)} fusion(bf16[128,16,512]{2,1,0:T(8,128)(2,1)} %get-tuple-element.4, s32[16]{0:T(128)S(1)} %multiply_add_fusion), kind=kOutput, calls=%fused_computation.12 | convolution fusion | flops 69207552 | bytes 6291520 | tf_op jit(solution)/shard_map/cb,rbf->crf/dot_general | solution.py:39
  32.5 7.9 %copy.55 = bf16[32,128,512]{1,2,0:T(8,128)(2,1)} copy(bf16[32,128,512]{2,0,1:T(8,128)(2,1)} %convolution_convert_fusion) | data formatting | bytes 8388608 | tf_op jit(solution)/shard_map/reshape | solution.py:40
  40.3 44.8 %all-to-all-done.1 = bf16[8,4,128,512]{3,2,1,0:T(8,128)(2,1)} async-done(((bf16[8,4,128,512]{3,2,1,0:T(8,128)(2,1)}), bf16[8,4,128,512]{3,2,1,0:T(8,128)(2,1)}, u32[]{:S(2)}, u32[]{:S(2)}) %all-to-all-start.1) | async-done | bytes 4194336 | tf_op jit(solution)/shard_map/all_to_all | solution.py:69
  85.1 6.9 %all-to-all-start.3 = ((bf16[8,4,128,512]{2,3,1,0:T(8,128)(2,1)}), bf16[8,4,128,512]{2,3,1,0:T(8,128)(2,1)}, u32[]{:S(2)}, u32[]{:S(2)}) async-start(bf16[8,4,128,512]{2,3,1,0:T(8,128)(2,1)} %bitcast.77), calls=%async_computation.3 | async-start | bytes 8388608 | tf_op jit(solution)/shard_map/all_to_all | solution.py:83
  92.0 4.9 %convolution_convert_fusion.1 = bf16[32,128,512]{2,0,1:T(8,128)(2,1)} fusion(bf16[128,16,512]{2,1,0:T(8,128)(2,1)} %get-tuple-element.6, s32[16]{0:T(128)S(1)} %multiply_add_fusion), kind=kOutput, calls=%fused_computation.13 | convolution fusion | flops 69207552 | bytes 6291520 | tf_op jit(solution)/shard_map/cb,rbf->crf/dot_general | solution.py:39
  97.0 7.9 %copy.54 = bf16[32,128,512]{1,2,0:T(8,128)(2,1)} copy(bf16[32,128,512]{2,0,1:T(8,128)(2,1)} %convolution_convert_fusion.1) | data formatting | bytes 8388608 | tf_op jit(solution)/shard_map/reshape | solution.py:40
  104.8 41.7 %all-to-all-done.3 = bf16[8,4,128,512]{2,3,1,0:T(8,128)(2,1)} async-done(((bf16[8,4,128,512]{2,3,1,0:T(8,128)(2,1)}), bf16[8,4,128,512]{2,3,1,0:T(8,128)(2,1)}, u32[]{:S(2)}, u32[]{:S(2)}) %all-to-all-start.3) | async-done | bytes 4194336 | tf_op jit(solution)/shard_map/all_to_all | solution.py:83
  146.5 8.7 %all-to-all-start.2 = ((bf16[8,4,128,512]{2,3,1,0:T(8,128)(2,1)}), bf16[8,4,128,512]{2,3,1,0:T(8,128)(2,1)}, u32[]{:S(2)}, u32[]{:S(2)}) async-start(bf16[8,4,128,512]{2,3,1,0:T(8,128)(2,1)} %bitcast.76), calls=%async_computation.2 | async-start | bytes 8388608 | tf_op jit(solution)/shard_map/all_to_all | solution.py:76
  156.6 4.4 %copy.52 = bf16[32,128,512]{2,1,0:T(8,128)(2,1)} copy(bf16[32,128,512]{2,0,1:T(8,128)(2,1)S(1)} %convolution_convert_fusion.3) | data formatting | bytes 8388608 | tf_op jit(solution)/shard_map/reshape | solution.py:40
  161.0 48.4 %all-to-all-done.2 = bf16[8,4,128,512]{2,3,1,0:T(8,128)(2,1)} async-done(((bf16[8,4,128,512]{2,3,1,0:T(8,128)(2,1)}), bf16[8,4,128,512]{2,3,1,0:T(8,128)(2,1)}, u32[]{:S(2)}, u32[]{:S(2)}) %all-to-all-start.2) | async-done | bytes 4194336 | tf_op jit(solution)/shard_map/all_to_all | solution.py:76
  209.4 8.7 %all-to-all-start = ((bf16[8,4,128,512]{3,2,1,0:T(8,128)(2,1)}), bf16[8,4,128,512]{3,2,1,0:T(8,128)(2,1)}, u32[]{:S(2)}, u32[]{:S(2)}) async-start(bf16[8,4,128,512]{3,2,1,0:T(8,128)(2,1)} %bitcast.75), calls=%async_computation | async-start | bytes 8388608 | tf_op jit(solution)/shard_map/all_to_all | solution.py:62
  218.1 4.6 %copy.46 = bf16[8,4,128,512]{2,3,0,1:T(8,128)(2,1)} copy(bf16[8,4,128,512]{2,3,1,0:T(8,128)(2,1)} %all-to-all-done.3) | data formatting | bytes 8388608 | tf_op jit(solution)/shard_map/all_to_all | solution.py:83
  224.6 4.7 %copy.43 = bf16[8,4,128,512]{2,3,0,1:T(8,128)(2,1)} copy(bf16[8,4,128,512]{2,3,1,0:T(8,128)(2,1)} %all-to-all-done.2) | data formatting | bytes 8388608 | tf_op jit(solution)/shard_map/all_to_all | solution.py:76
  229.2 4.1 %collective-permute-start = (bf16[8,4,128,512]{2,3,0,1:T(8,128)(2,1)}, bf16[8,4,128,512]{2,3,0,1:T(8,128)(2,1)}, u32[]{:S(2)}, u32[]{:S(2)}) collective-permute-start(bf16[8,4,128,512]{2,3,0,1:T(8,128)(2,1)} %copy.43), channel_id=1, source_target_pairs={{0,8},{8,16},{16,24},{24,32},{32,40},{40,48},{48,56},{56,64},{64,7... | collective-permute-start | bytes 12582920 | tf_op jit(solution)/shard_map/ppermute | solution.py:10
  233.4 7.9 %convolution_bitcast_fusion = f32[1,1,4,512,512]{4,3,2,1,0:T(8,128)} fusion(bf16[8,4,128,512]{3,2,1,0:T(8,128)(2,1)} %all-to-all-done.1), kind=kOutput, calls=%fused_computation.18 | convolution fusion | flops 2147483648 | bytes 8388608 | tf_op jit(solution)/shard_map/gkrf,gkrh->kfh/dot_general | solution.py:44
  241.3 30.9 %all-to-all-done = bf16[8,4,128,512]{3,2,1,0:T(8,128)(2,1)} async-done(((bf16[8,4,128,512]{3,2,1,0:T(8,128)(2,1)}), bf16[8,4,128,512]{3,2,1,0:T(8,128)(2,1)}, u32[]{:S(2)}, u32[]{:S(2)}) %all-to-all-start) | async-done | bytes 4194336 | tf_op jit(solution)/shard_map/all_to_all | solution.py:62
  272.2 7.9 %convolution_bitcast_fusion.1 = f32[1,1,4,512,512]{4,3,2,1,0:T(8,128)} fusion(bf16[8,4,128,512]{3,2,1,0:T(8,128)(2,1)} %all-to-all-done), kind=kOutput, calls=%fused_computation.19 | convolution fusion | flops 2147483648 | bytes 8388608 | tf_op jit(solution)/shard_map/gkrf,gkrh->kfh/dot_general | solution.py:44
  280.0 31.3 %collective-permute-done.1 = bf16[8,4,128,512]{2,3,0,1:T(8,128)(2,1)} collective-permute-done((bf16[8,4,128,512]{2,3,0,1:T(8,128)(2,1)}, bf16[8,4,128,512]{2,3,0,1:T(8,128)(2,1)}, u32[]{:S(2)}, u32[]{:S(2)}) %collective-permute-start.1) | collective-permute-done | bytes 4194336 | tf_op jit(solution)/shard_map/ppermute | solution.py:10
  311.3 7.8 %fusion.11 = f32[1,1,4,512,512]{4,3,2,1,0:T(8,128)} fusion(bf16[8,4,128,512]{2,3,0,1:T(8,128)(2,1)} %collective-permute-done.1, bf16[8,4,128,512]{3,2,1,0:T(8,128)(2,1)} %all-to-all-done.1), kind=kOutput, calls=%fused_computation.17 | convolution fusion | flops 2147483648 | bytes 12582912 | tf_op jit(solution)/shard_map/gkrf,gkrh->kfh/dot_general | solution.py:44
  319.1 37.1 %collective-permute-done = bf16[8,4,128,512]{2,3,0,1:T(8,128)(2,1)} collective-permute-done((bf16[8,4,128,512]{2,3,0,1:T(8,128)(2,1)}, bf16[8,4,128,512]{2,3,0,1:T(8,128)(2,1)}, u32[]{:S(2)}, u32[]{:S(2)}) %collective-permute-start) | collective-permute-done | bytes 4194336 | tf_op jit(solution)/shard_map/ppermute | solution.py:10
  356.3 7.8 %fusion.8 = f32[1,1,4,512,512]{4,3,2,1,0:T(8,128)} fusion(bf16[8,4,128,512]{2,3,0,1:T(8,128)(2,1)} %collective-permute-done, bf16[8,4,128,512]{3,2,1,0:T(8,128)(2,1)} %all-to-all-done), kind=kOutput, calls=%fused_computation.16 | convolution fusion | flops 2147483648 | bytes 12582912 | tf_op jit(solution)/shard_map/gkrf,gkrh->kfh/dot_general | solution.py:44
  (24 shorter events, 13.1 us)
Async XLA Ops:
  0.6 4.9 %copy-start = (bf16[1,128,8192]{2,1,0:T(8,128)(2,1)S(1)}, bf16[1,128,8192]{2,1,0:T(8,128)(2,1)}, u32[]{:S(2)}) copy-start(bf16[1,128,8192]{2,1,0:T(8,128)(2,1)} %param.7) | copy-start | bytes 6291460
  5.5 1.6 copy-start.1
  6.4 1.8 copy-start.2
  8.0 1.0 copy-start.3
  20.3 64.8 %all-to-all-start.1 = ((bf16[8,4,128,512]{3,2,1,0:T(8,128)(2,1)}), bf16[8,4,128,512]{3,2,1,0:T(8,128)(2,1)}, u32[]{:S(2)}, u32[]{:S(2)}) async-start(bf16[8,4,128,512]{3,2,1,0:T(8,128)(2,1)} %bitcast.78), calls=%async_computation.1 | async-start | bytes 8388608 | tf_op jit(solution)/shard_map/all_to_all | solution.py:69
  85.1 61.4 %all-to-all-start.3 = ((bf16[8,4,128,512]{2,3,1,0:T(8,128)(2,1)}), bf16[8,4,128,512]{2,3,1,0:T(8,128)(2,1)}, u32[]{:S(2)}, u32[]{:S(2)}) async-start(bf16[8,4,128,512]{2,3,1,0:T(8,128)(2,1)} %bitcast.77), calls=%async_computation.3 | async-start | bytes 8388608 | tf_op jit(solution)/shard_map/all_to_all | solution.py:83
  146.5 62.9 %all-to-all-start.2 = ((bf16[8,4,128,512]{2,3,1,0:T(8,128)(2,1)}), bf16[8,4,128,512]{2,3,1,0:T(8,128)(2,1)}, u32[]{:S(2)}, u32[]{:S(2)}) async-start(bf16[8,4,128,512]{2,3,1,0:T(8,128)(2,1)} %bitcast.76), calls=%async_computation.2 | async-start | bytes 8388608 | tf_op jit(solution)/shard_map/all_to_all | solution.py:76
  209.4 62.8 %all-to-all-start = ((bf16[8,4,128,512]{3,2,1,0:T(8,128)(2,1)}), bf16[8,4,128,512]{3,2,1,0:T(8,128)(2,1)}, u32[]{:S(2)}, u32[]{:S(2)}) async-start(bf16[8,4,128,512]{3,2,1,0:T(8,128)(2,1)} %bitcast.75), calls=%async_computation | async-start | bytes 8388608 | tf_op jit(solution)/shard_map/all_to_all | solution.py:62
  222.7 88.7 %collective-permute-start.1 = (bf16[8,4,128,512]{2,3,0,1:T(8,128)(2,1)}, bf16[8,4,128,512]{2,3,0,1:T(8,128)(2,1)}, u32[]{:S(2)}, u32[]{:S(2)}) collective-permute-start(bf16[8,4,128,512]{2,3,0,1:T(8,128)(2,1)} %copy.46), channel_id=1, source_target_pairs={{0,8},{8,16},{16,24},{24,32},{32,40},{40,48},{48,56},{56,64},{64,7... | collective-permute-start | bytes 12582920 | tf_op jit(solution)/shard_map/ppermute | solution.py:10
  229.2 127.0 %collective-permute-start = (bf16[8,4,128,512]{2,3,0,1:T(8,128)(2,1)}, bf16[8,4,128,512]{2,3,0,1:T(8,128)(2,1)}, u32[]{:S(2)}, u32[]{:S(2)}) collective-permute-start(bf16[8,4,128,512]{2,3,0,1:T(8,128)(2,1)} %copy.43), channel_id=1, source_target_pairs={{0,8},{8,16},{16,24},{24,32},{32,40},{40,48},{48,56},{56,64},{64,7... | collective-permute-start | bytes 12582920 | tf_op jit(solution)/shard_map/ppermute | solution.py:10
where the time goes:
time: 365 us; the launch traced here: 364 us
  waiting for transfers between devices  234 us (64%)
  matrix products  43.9 us (12%)
  local copies, waits for them, and re-layouts  40.4 us (11%)
  starting transfers between devices  37.5 us (10%)
  other arithmetic  7.29 us (2%)
    ppermute x2, waiting for transfers between devices, shifted(): return lax.ppermute(block, axis, route)  68.4 us
    all_to_all x1, waiting for transfers between devices, on_device(): lax.all_to_all(into_slots(tail_acts, selector, groups, slot_count), 'dp',...  48.4 us
    all_to_all x1, waiting for transfers between devices, on_device(): lax.all_to_all(into_slots(own_grads, selector, groups, slot_count), 'dp',...  44.8 us
    all_to_all x1, waiting for transfers between devices, on_device(): lax.all_to_all(into_slots(tail_grads, selector, groups, slot_count), 'dp'...  41.7 us
    dot_general x4, matrix products, owner_gram(): jnp.einsum('gkrf,gkrh->kfh', former, latter, preferred_element_type=jnp.f...  31.3 us
    all_to_all x1, waiting for transfers between devices, on_device(): lax.all_to_all(into_slots(own_acts, selector, groups, slot_count), 'dp',...  30.9 us
    reshape x4, local copies, waits for them, and re-layouts, into_slots(): placed.astype(jnp.bfloat16)  24.5 us
    dot_general x4, matrix products, into_slots(): jnp.einsum('cb,rbf->crf', selector, blocked, preferred_element_type=jnp.f...  12.6 us
  transfers between devices with their start and end apart: 6, of which 6 were waited for; matrix products, arithmetic and copies ran while one was open for 18% of the time, Pallas kernels for 0%

commit v1 on v0

v1 whole, which is shorter than its diff:
```python
import functools

import jax
import jax.numpy as jnp
from jax import lax
from jax.experimental import pallas as pl
from jax.experimental.pallas import tpu as pltpu
from jax.sharding import PartitionSpec as P

FB = 512
KEEP = 2


def row_scale(doc_lengths, row_count, docs_all):
    doc_sizes = doc_lengths.astype(jnp.float32)
    doc_end = jnp.cumsum(doc_lengths)
    starts = doc_end - doc_lengths
    places = jnp.arange(row_count, dtype=jnp.int32)
    inside = (places[:, None] >= starts[None, :]) & (places[:, None] < doc_end[None, :])
    inverse = jnp.sum(jnp.where(inside, 1.0 / doc_sizes[None, :], jnp.float32(0.0)), axis=1)
    return jnp.sqrt(inverse / docs_all)


def placement(block_owner, groups):
    blocks = block_owner.shape[0]
    position = jnp.arange(blocks, dtype=jnp.int32)
    same_owner = block_owner[:, None] == block_owner[None, :]
    slot = jnp.sum(jnp.where(same_owner & (position[None, :] < position[:, None]), 1, 0), axis=1)
    owned = jnp.sum(jnp.where(block_owner[:, None] == jnp.arange(groups)[None, :], 1, 0), axis=0)
    group = jnp.arange(groups, dtype=jnp.int32)
    spare = jnp.sum(jnp.where(owned == 0, group, 0))
    full = jnp.sum(jnp.where(owned > KEEP, group, 0))
    target = jnp.where(slot < KEEP, block_owner, spare) * KEEP + slot % KEEP
    order = jnp.sum(jnp.where(target[None, :] == position[:, None], position[None, :], 0), axis=1)
    return order.astype(jnp.int32), spare.astype(jnp.int32), full.astype(jnp.int32)


def scale_kernel(order, weight, fa, fg, la, lg, f_out, la_out, lg_out):
    w = weight[...]

    def scaled(ref):
        return (ref[...].astype(jnp.float32) * w).astype(jnp.bfloat16)

    f_out[0, 0, 0] = scaled(fa)
    f_out[0, 1, 0] = scaled(fg)
    la_out[0, 0] = scaled(la)
    lg_out[0, 0] = scaled(lg)


def scale_and_sort(order, weight, fa, fg, la, lg, groups):
    rows = fa.shape[0]
    blocks = groups * KEEP
    column = pl.BlockSpec((rows, FB), lambda i, o: (0, o[i]))
    return pl.pallas_call(
        scale_kernel,
        grid_spec=pltpu.PrefetchScalarGridSpec(
            num_scalar_prefetch=1,
            grid=(blocks,),
            in_specs=[pl.BlockSpec((rows, 1), lambda i, o: (0, 0))] + [column] * 4,
            out_specs=[
                pl.BlockSpec((1, 2, 1, rows, FB), lambda i, o: (i // KEEP, 0, i % KEEP, 0, 0)),
                pl.BlockSpec((1, 1, rows, FB), lambda i, o: (i // KEEP, i % KEEP, 0, 0)),
                pl.BlockSpec((1, 1, rows, FB), lambda i, o: (i // KEEP, i % KEEP, 0, 0)),
            ],
        ),
        out_shape=[
            jax.ShapeDtypeStruct((groups, 2, KEEP, rows, FB), jnp.bfloat16),
            jax.ShapeDtypeStruct((groups, KEEP, rows, FB), jnp.bfloat16),
            jax.ShapeDtypeStruct((groups, KEEP, rows, FB), jnp.bfloat16),
        ],
        name="scale_sort",
    )(order, weight, fa, fg, la, lg)


def gram(x, y):
    return lax.dot_general(x, y, (((0,), (0,)), ((), ())), preferred_element_type=jnp.float32)


def factor_kernel(mine, f_in, a_out, g_out, hand):
    k = pl.program_id(0)

    @pl.when(k < KEEP)
    def _():
        keep = mine[0] != 0
        for a, out in ((0, a_out), (1, g_out)):
            x = f_in[:, a, 0].reshape(-1, FB)
            r = gram(x, x)
            out[0] = jnp.where(keep, r, 0.0)
            hand[a, 0] = r.astype(jnp.bfloat16)

    @pl.when(k >= KEEP)
    def _():
        a_out[...] = jnp.zeros_like(a_out)
        g_out[...] = jnp.zeros_like(g_out)


def factors(mine, f_in):
    groups, _, _, rows, _ = f_in.shape
    out = jax.ShapeDtypeStruct((2 * KEEP, FB, FB), jnp.float32)
    return pl.pallas_call(
        factor_kernel,
        grid_spec=pltpu.PrefetchScalarGridSpec(
            num_scalar_prefetch=1,
            grid=(2 * KEEP,),
            in_specs=[
                pl.BlockSpec(
                    (groups, 2, 1, rows, FB), lambda k, m: (0, 0, jnp.minimum(k, KEEP - 1), 0, 0)
                )
            ],
            out_specs=[
                pl.BlockSpec((1, FB, FB), lambda k, m: (k, 0, 0)),
                pl.BlockSpec((1, FB, FB), lambda k, m: (k, 0, 0)),
                pl.BlockSpec(
                    (2, 1, FB, FB), lambda k, m: (0, jnp.minimum(k, KEEP - 1), 0, 0)
                ),
            ],
        ),
        out_shape=[out, out, jax.ShapeDtypeStruct((2, KEEP, FB, FB), jnp.bfloat16)],
        compiler_params=pltpu.CompilerParams(vmem_limit_bytes=48 << 20),
        name="factor_gram",
    )(mine, f_in)


def cross_kernel(swap_pairs, mine, l_in, f_in, out, hand):
    k = pl.program_id(0)

    @pl.when(k < KEEP)
    def _():
        keep = mine[0] != 0
        last = l_in[:, 0]
        groups, rows, _ = last.shape
        if swap_pairs:
            pairs = last.reshape(groups // 2, 2, rows, FB)
            turned = jnp.concatenate([pairs[:, 1:], pairs[:, :1]], axis=1).reshape(last.shape)
            last = jnp.where(mine[1] != 0, turned, last)
        r = gram(last.reshape(-1, FB), f_in[:, 0, 0].reshape(-1, FB))
        out[0] = jnp.where(keep, r, 0.0)
        hand[0] = r.astype(jnp.bfloat16)

    @pl.when(k >= KEEP)
    def _():
        out[...] = jnp.zeros_like(out)


def cross(mine, l_in, f_in, which, swap_pairs):
    groups, _, rows, _ = l_in.shape
    return pl.pallas_call(
        functools.partial(cross_kernel, swap_pairs),
        grid_spec=pltpu.PrefetchScalarGridSpec(
            num_scalar_prefetch=1,
            grid=(2 * KEEP,),
            in_specs=[
                pl.BlockSpec((groups, 1, rows, FB), lambda k, m: (0, jnp.minimum(k, KEEP - 1), 0, 0)),
                pl.BlockSpec(
                    (groups, 1, 1, rows, FB),
                    lambda k, m: (0, which, jnp.minimum(k, KEEP - 1), 0, 0),
                ),
            ],
            out_specs=[
                pl.BlockSpec((1, FB, FB), lambda k, m: (k, 0, 0)),
                pl.BlockSpec((1, FB, FB), lambda k, m: (jnp.minimum(k, KEEP - 1), 0, 0)),
            ],
        ),
        out_shape=[
            jax.ShapeDtypeStruct((2 * KEEP, FB, FB), jnp.float32),
            jax.ShapeDtypeStruct((KEEP, FB, FB), jnp.bfloat16),
        ],
        compiler_params=pltpu.CompilerParams(vmem_limit_bytes=48 << 20),
        name="cross_gram",
    )(mine, l_in, f_in)


def fill_kernel(flag, got, old, out, half, wide, sem):
    @pl.when(flag[0] != 0)
    def _():
        load = pltpu.make_async_copy(got, half, sem)
        load.start()
        load.wait()
        wide[...] = half[...].astype(jnp.float32)
        store = pltpu.make_async_copy(wide, out.at[pl.ds(KEEP, KEEP)], sem)
        store.start()
        store.wait()


def fill(flag, got, old):
    return pl.pallas_call(
        fill_kernel,
        in_specs=[
            pl.BlockSpec(memory_space=pltpu.SMEM),
            pl.BlockSpec(memory_space=pl.ANY),
            pl.BlockSpec(memory_space=pl.ANY),
        ],
        out_specs=pl.BlockSpec(memory_space=pl.ANY),
        out_shape=jax.ShapeDtypeStruct(old.shape, old.dtype),
        scratch_shapes=[
            pltpu.VMEM(got.shape, jnp.bfloat16),
            pltpu.VMEM(got.shape, jnp.float32),
            pltpu.SemaphoreType.DMA,
        ],
        input_output_aliases={2: 0},
        name="fill_slots",
    )(flag, got, old)


def hand_over(route, groups, *blocks):
    axes = ("section", "dp")
    sections = lax.axis_size("section")

    def along(spare, full, *values):
        pairs = [(s * groups + spare, s * groups + full) for s in range(sections)]
        return tuple(lax.ppermute(v, axes, pairs) for v in values)

    cases = [(s, f) for s in range(1, groups - 1) for f in range(groups) if f != s]
    return lax.switch(route, [functools.partial(along, s, f) for s, f in cases], *blocks)


def on_device(first_acts, first_grads, last_acts, last_grads, doc_lengths, block_owner):
    row_count = first_acts.shape[1]
    groups = lax.axis_size("dp")
    sections = lax.axis_size("section")
    axes = ("section", "dp")
    me = lax.axis_index("dp")
    section = lax.axis_index("section")
    weight = row_scale(doc_lengths[0], row_count, doc_lengths.shape[1] * groups)[:, None]
    order, spare, full = placement(block_owner, groups)
    route = (spare - 1) * (groups - 1) + full - jnp.where(full > spare, 1, 0)
    boundary = sections // 2
    mine = jnp.stack([me != spare, section == boundary]).astype(jnp.int32)
    receive = (me == full).astype(jnp.int32).reshape(1)

    f, la, lg = scale_and_sort(
        order, weight, first_acts[0], first_grads[0], last_acts[0], last_grads[0], groups
    )
    straight = [(s * groups + d, (s + 1) * groups + d) for s in range(sections - 1) for d in range(groups)]
    turned = [
        (s * groups + d, (s + 1) * groups + (d ^ 1 if s + 1 == boundary else d))
        for s in range(sections - 1)
        for d in range(groups)
    ]
    la = lax.ppermute(la, axes, straight)
    lg = lax.ppermute(lg, axes, turned)

    def exchange(x):
        return lax.all_to_all(x, "dp", split_axis=0, concat_axis=0, tiled=True)

    f_in = exchange(f)
    la_in = exchange(la)
    lg_in = exchange(lg)
    af, gf, f_hand = factors(mine, f_in)
    ac, ac_hand = cross(mine, la_in, f_in, 0, False)
    gc, gc_hand = cross(mine, lg_in, f_in, 1, True)
    (f_got,) = hand_over(route, groups, f_hand)
    (ac_got,) = hand_over(route, groups, ac_hand)
    (gc_got,) = hand_over(route, groups, gc_hand)
    af = fill(receive, f_got[0], af)
    gf = fill(receive, f_got[1], gf)
    ac = fill(receive, ac_got, ac)
    gc = fill(receive, gc_got, gc)
    return af[None, None], gf[None, None], ac[None, None], gc[None, None]


def solution(mesh):
    placed = (
        P("section", "dp", None),
        P("section", "dp", None),
        P("section", "dp", None),
        P("section", "dp", None),
        P("dp", None),
        P(),
    )
    return jax.shard_map(
        on_device,
        mesh=mesh,
        in_specs=placed,
        out_specs=(P("section", "dp", None, None, None),) * 4,
        check_vma=False,
    )
```

time: 365 us -> 346 us (0.948)
  the two profiles are of different devices: /device:TPU:30 before, /device:TPU:14 now
where the time goes in v1:
time: 346 us
  waiting for transfers between devices  211 us (61%)
  starting transfers between devices  80.4 us (23%)
  Pallas kernels  32 us (9%)
  local copies, waits for them, and re-layouts  11.2 us (3%)
  other arithmetic  5.96 us (2%)
  between operations  4.72 us (1%)
    ppermute x1, waiting for transfers between devices, on_device(): lg = lax.ppermute(lg, axes, turned)  106 us
    ppermute x3, waiting for transfers between devices, along(): return tuple((lax.ppermute(v, axes, pairs) for v in values))  89.4 us
    ppermute x3, starting transfers between devices, along(): return tuple((lax.ppermute(v, axes, pairs) for v in values))  38.9 us
    all_to_all x3, starting transfers between devices, exchange(): return lax.all_to_all(x, 'dp', split_axis=0, concat_axis=0, tiled=True)  19.8 us
    all_to_all x3, waiting for transfers between devices, exchange(): return lax.all_to_all(x, 'dp', split_axis=0, concat_axis=0, tiled=True)  15.9 us
    pallas_call x1, Pallas kernels, scale_and_sort(): pl.pallas_call(scale_kernel, grid_spec=pltpu.PrefetchScalarGridSpec(num_s...  13.6 us
    ppermute x1, starting transfers between devices, on_device(): lg = lax.ppermute(lg, axes, turned)  11.5 us
    pallas_call x2, Pallas kernels, cross(): pl.pallas_call(functools.partial(cross_kernel, swap_pairs), grid_spec=plt...  10.8 us
  transfers between devices with their start and end apart: 8, of which 5 were waited for; matrix products, arithmetic and copies ran while one was open for 1% of the time, Pallas kernels for 4%

profile of v1, /device:TPU:14, one launch (start us, length us, event | category | flops | bytes accessed | tf_op | source)
XLA Modules:
  0.0 346.1 jit_solution(9017483061652642619)
XLA Ops:
  8.0 13.6 %scale_sort.1 = (bf16[8,2,2,128,512]{4,3,2,1,0:T(8,128)(2,1)}, bf16[8,2,128,512]{3,2,1,0:T(8,128)(2,1)}, bf16[8,2,128,512]{3,2,1,0:T(8,128)(2,1)}) custom-call(s32[16]{0:T(128)} %select_reduce_fusion.1.order, f32[128,1]{1,0:T(8,128)} %copy.19.weight, bf16[128,8192]{1,0:T(8,128)(2,1)} %bitcast.110, bf16[128,8192]{1,0:T(8,128)(2,1)} %bitcast.111, ...), custom_call_target="tpu_custom_call" | custom-call | tf_op jit(solution)/shard_map/scale_sort/pallas_call | solution.py:54
  21.6 6.5 %all-to-all-start = ((bf16[8,2,2,128,512]{4,3,2,1,0:T(8,128)(2,1)}), bf16[8,2,2,128,512]{4,3,2,1,0:T(8,128)(2,1)}, u32[]{:S(2)}, u32[]{:S(2)}) async-start(bf16[8,2,2,128,512]{4,3,2,1,0:T(8,128)(2,1)} %get-tuple-element.233), calls=%async_computation | async-start | bytes 8388608 | tf_op jit(solution)/shard_map/all_to_all | solution.py:244
  28.1 11.5 %collective-permute-start.127 = (bf16[8,2,128,512]{3,2,1,0:T(8,128)(2,1)}, bf16[8,2,128,512]{3,2,1,0:T(8,128)(2,1)S(1)}, u32[]{:S(2)}, u32[]{:S(2)}) collective-permute-start(bf16[8,2,128,512]{3,2,1,0:T(8,128)(2,1)} %get-tuple-element.242), channel_id=1, source_target_pairs={{0,8},{1,9},{2,10},{3,11},{4,12},{5,13},{6,14},{7,15},{8,16},{9,17... | collective-permute-start | bytes 6291464 | tf_op jit(solution)/shard_map/ppermute | solution.py:241
  39.6 10.2 %collective-permute-start.126 = (bf16[8,2,128,512]{3,2,1,0:T(8,128)(2,1)}, bf16[8,2,128,512]{3,2,1,0:T(8,128)(2,1)}, u32[]{:S(2)}, u32[]{:S(2)}) collective-permute-start(bf16[8,2,128,512]{3,2,1,0:T(8,128)(2,1)} %get-tuple-element.239), channel_id=1, source_target_pairs={{0,8},{1,9},{2,10},{3,11},{4,12},{5,13},{6,14},{7,15},{8,16},{9,17... | collective-permute-start | bytes 6291464 | tf_op jit(solution)/shard_map/ppermute | solution.py:240
  49.7 105.9 %collective-permute-done.127 = bf16[8,2,128,512]{3,2,1,0:T(8,128)(2,1)S(1)} collective-permute-done((bf16[8,2,128,512]{3,2,1,0:T(8,128)(2,1)}, bf16[8,2,128,512]{3,2,1,0:T(8,128)(2,1)S(1)}, u32[]{:S(2)}, u32[]{:S(2)}) %collective-permute-start.127) | collective-permute-done | bytes 2097184 | tf_op jit(solution)/shard_map/ppermute | solution.py:241
  155.7 1.3 copy-done.44
  157.0 6.1 %all-to-all-start.2 = ((bf16[8,2,128,512]{3,2,1,0:T(8,128)(2,1)}), bf16[8,2,128,512]{3,2,1,0:T(8,128)(2,1)S(1)}, u32[]{:S(2)}, u32[]{:S(2)}) async-start(bf16[8,2,128,512]{3,2,1,0:T(8,128)(2,1)} %copy-done.44), calls=%async_computation.2 | async-start | bytes 4194304 | tf_op jit(solution)/shard_map/all_to_all | solution.py:244
  163.1 15.9 %all-to-all-done.2.l_in = bf16[8,2,128,512]{3,2,1,0:T(8,128)(2,1)S(1)} async-done(((bf16[8,2,128,512]{3,2,1,0:T(8,128)(2,1)}), bf16[8,2,128,512]{3,2,1,0:T(8,128)(2,1)S(1)}, u32[]{:S(2)}, u32[]{:S(2)}) %all-to-all-start.2) | async-done | bytes 2097184 | tf_op jit(solution)/shard_map/all_to_all | solution.py:244
  180.3 7.3 %all-to-all-start.1 = ((bf16[8,2,128,512]{3,2,1,0:T(8,128)(2,1)}), bf16[8,2,128,512]{3,2,1,0:T(8,128)(2,1)S(1)}, u32[]{:S(2)}, u32[]{:S(2)}) async-start(bf16[8,2,128,512]{3,2,1,0:T(8,128)(2,1)} %collective-permute-done.126), calls=%async_computation.1 | async-start | bytes 4194304 | tf_op jit(solution)/shard_map/all_to_all | solution.py:244
  191.5 7.6 %factor_gram.1 = (f32[4,512,512]{2,1,0:T(8,128)}, f32[4,512,512]{2,1,0:T(8,128)}, bf16[2,2,512,512]{3,2,1,0:T(8,128)(2,1)S(1)}) custom-call(s32[2]{0:T(128)S(1)} %add_convert_fusion.mine, bf16[8,2,2,128,512]{4,3,2,1,0:T(8,128)(2,1)} %all-to-all-done.f_in), custom_call_target="tpu_custom_call" | custom-call | tf_op jit(solution)/shard_map/factor_gram/pallas_call | solution.py:100
  199.0 59.4 %conditional.3 = (bf16[2,2,512,512]{3,2,1,0:T(8,128)(2,1)}, bf16[1,2,512,512]{3,2,1,0:T(8,128)(2,1)}, bf16[1,2,512,512]{3,2,1,0:T(8,128)(2,1)}, bf16[2,512,512]{2,1,0:T(8,128)(2,1)S(1)}, bf16[2,512,512]{2,1,0:T(8,128)(2,1)}) conditional(s32[]{:T(128)} %clamp.2, ...), branch_computations={%region_7.8_spmd, %region_8.9_spmd, %region_9.10_spmd, %region_10.... | conditional | bytes 25165932 | solution.py:214
  199.4 8.0 %collective-permute-start.124 = (bf16[2,2,512,512]{3,2,1,0:T(8,128)(2,1)S(1)}, bf16[2,2,512,512]{3,2,1,0:T(8,128)(2,1)S(1)}, u32[]{:S(2)}, u32[]{:S(2)}) collective-permute-start(bf16[2,2,512,512]{3,2,1,0:T(8,128)(2,1)S(1)} %param.40), channel_id=1, source_target_pairs={{6,5},{14,13},{22,21},{30,29},{38,37},{46,45},{54,53},{62,61},{70,... | collective-permute-start | bytes 6291464 | tf_op jit(solution)/shard_map/cond/branch_40_fun/ppermute | solution.py:211
  207.4 45.3 %collective-permute-done.124 = bf16[2,2,512,512]{3,2,1,0:T(8,128)(2,1)S(1)} collective-permute-done((bf16[2,2,512,512]{3,2,1,0:T(8,128)(2,1)S(1)}, bf16[2,2,512,512]{3,2,1,0:T(8,128)(2,1)S(1)}, u32[]{:S(2)}, u32[]{:S(2)}) %collective-permute-start.124) | collective-permute-done | bytes 2097184 | tf_op jit(solution)/shard_map/cond/branch_40_fun/ppermute | solution.py:211
  252.7 1.5 fusion.48
  255.9 2.3 copy.224
  258.5 1.6 copy-done.1
  260.0 5.4 %cross_gram.3 = (f32[4,512,512]{2,1,0:T(8,128)}, bf16[2,512,512]{2,1,0:T(8,128)(2,1)S(1)}) custom-call(s32[2]{0:T(128)S(1)} %add_convert_fusion.mine, bf16[8,2,128,512]{3,2,1,0:T(8,128)(2,1)S(1)} %copy-done.1, bf16[8,2,2,128,512]{4,3,2,1,0:T(8,128)(2,1)} %all-to-all-done.f_in), custom_call_target="tpu_custom_call" | custom-call | tf_op jit(solution)/shard_map/cross_gram/pallas_call | solution.py:147
  265.4 39.5 %conditional.5 = (bf16[2,512,512]{2,1,0:T(8,128)(2,1)}) conditional(s32[]{:T(128)} %clamp.2, bf16[2,512,512]{2,1,0:T(8,128)(2,1)S(1)} %get-tuple-element.243, bf16[2,512,512]{2,1,0:T(8,128)(2,1)S(1)} %get-tuple-element.243, bf16[2,512,512]{2,1,0:T(8,128)(2,1)S(1)} %get-tuple-element.243, ...), branch_computations={%region_91.92_spmd, %region_92.93_spmd, %region_93.94_spmd, %regio... | conditional | bytes 4194352 | solution.py:214
  265.4 17.5 %collective-permute-start.82 = (bf16[2,512,512]{2,1,0:T(8,128)(2,1)S(1)}, bf16[2,512,512]{2,1,0:T(8,128)(2,1)}, u32[]{:S(2)}, u32[]{:S(2)}) collective-permute-start(bf16[2,512,512]{2,1,0:T(8,128)(2,1)S(1)} %param.124), channel_id=1, source_target_pairs={{6,5},{14,13},{22,21},{30,29},{38,37},{46,45},{54,53},{62,61},{70,... | collective-permute-start | bytes 3145736 | tf_op jit(solution)/shard_map/cond/branch_40_fun/ppermute | solution.py:211
  282.9 22.0 %collective-permute-done.82 = bf16[2,512,512]{2,1,0:T(8,128)(2,1)} collective-permute-done((bf16[2,512,512]{2,1,0:T(8,128)(2,1)S(1)}, bf16[2,512,512]{2,1,0:T(8,128)(2,1)}, u32[]{:S(2)}, u32[]{:S(2)}) %collective-permute-start.82) | collective-permute-done | bytes 1048608 | tf_op jit(solution)/shard_map/cond/branch_40_fun/ppermute | solution.py:211
  305.0 5.4 %cross_gram.2 = (f32[4,512,512]{2,1,0:T(8,128)}, bf16[2,512,512]{2,1,0:T(8,128)(2,1)S(1)}) custom-call(s32[2]{0:T(128)S(1)} %add_convert_fusion.mine, bf16[8,2,128,512]{3,2,1,0:T(8,128)(2,1)S(1)} %all-to-all-done.1.l_in, bf16[8,2,2,128,512]{4,3,2,1,0:T(8,128)(2,1)} %all-to-all-done.f_in), custom_call_target="tpu_custom_call" | custom-call | tf_op jit(solution)/shard_map/cross_gram/pallas_call | solution.py:147
  310.4 35.5 %conditional.4 = (bf16[2,512,512]{2,1,0:T(8,128)(2,1)}) conditional(s32[]{:T(128)} %clamp.2, bf16[2,512,512]{2,1,0:T(8,128)(2,1)S(1)} %get-tuple-element.240, bf16[2,512,512]{2,1,0:T(8,128)(2,1)S(1)} %get-tuple-element.240, bf16[2,512,512]{2,1,0:T(8,128)(2,1)S(1)} %get-tuple-element.240, ...), branch_computations={%region_49.50_spmd, %region_50.51_spmd, %region_51.52_spmd, %regio... | conditional | bytes 4194352 | solution.py:214
  310.4 13.5 %collective-permute-start.40 = (bf16[2,512,512]{2,1,0:T(8,128)(2,1)S(1)}, bf16[2,512,512]{2,1,0:T(8,128)(2,1)}, u32[]{:S(2)}, u32[]{:S(2)}) collective-permute-start(bf16[2,512,512]{2,1,0:T(8,128)(2,1)S(1)} %param.82), channel_id=1, source_target_pairs={{6,5},{14,13},{22,21},{30,29},{38,37},{46,45},{54,53},{62,61},{70,... | collective-permute-start | bytes 3145736 | tf_op jit(solution)/shard_map/cond/branch_40_fun/ppermute | solution.py:211
  323.8 22.0 %collective-permute-done.40 = bf16[2,512,512]{2,1,0:T(8,128)(2,1)} collective-permute-done((bf16[2,512,512]{2,1,0:T(8,128)(2,1)S(1)}, bf16[2,512,512]{2,1,0:T(8,128)(2,1)}, u32[]{:S(2)}, u32[]{:S(2)}) %collective-permute-start.40) | collective-permute-done | bytes 1048608 | tf_op jit(solution)/shard_map/cond/branch_40_fun/ppermute | solution.py:211
  (28 shorter events, 10.5 us)
Async XLA Ops:
  21.6 135.4 %all-to-all-start = ((bf16[8,2,2,128,512]{4,3,2,1,0:T(8,128)(2,1)}), bf16[8,2,2,128,512]{4,3,2,1,0:T(8,128)(2,1)}, u32[]{:S(2)}, u32[]{:S(2)}) async-start(bf16[8,2,2,128,512]{4,3,2,1,0:T(8,128)(2,1)} %get-tuple-element.233), calls=%async_computation | async-start | bytes 8388608 | tf_op jit(solution)/shard_map/all_to_all | solution.py:244
  28.1 127.6 %collective-permute-start.127 = (bf16[8,2,128,512]{3,2,1,0:T(8,128)(2,1)}, bf16[8,2,128,512]{3,2,1,0:T(8,128)(2,1)S(1)}, u32[]{:S(2)}, u32[]{:S(2)}) collective-permute-start(bf16[8,2,128,512]{3,2,1,0:T(8,128)(2,1)} %get-tuple-element.242), channel_id=1, source_target_pairs={{0,8},{1,9},{2,10},{3,11},{4,12},{5,13},{6,14},{7,15},{8,16},{9,17... | collective-permute-start | bytes 6291464 | tf_op jit(solution)/shard_map/ppermute | solution.py:241
  39.6 123.5 %collective-permute-start.126 = (bf16[8,2,128,512]{3,2,1,0:T(8,128)(2,1)}, bf16[8,2,128,512]{3,2,1,0:T(8,128)(2,1)}, u32[]{:S(2)}, u32[]{:S(2)}) collective-permute-start(bf16[8,2,128,512]{3,2,1,0:T(8,128)(2,1)} %get-tuple-element.239), channel_id=1, source_target_pairs={{0,8},{1,9},{2,10},{3,11},{4,12},{5,13},{6,14},{7,15},{8,16},{9,17... | collective-permute-start | bytes 6291464 | tf_op jit(solution)/shard_map/ppermute | solution.py:240
  155.7 1.3 copy-start.44
  157.0 22.0 %all-to-all-start.2 = ((bf16[8,2,128,512]{3,2,1,0:T(8,128)(2,1)}), bf16[8,2,128,512]{3,2,1,0:T(8,128)(2,1)S(1)}, u32[]{:S(2)}, u32[]{:S(2)}) async-start(bf16[8,2,128,512]{3,2,1,0:T(8,128)(2,1)} %copy-done.44), calls=%async_computation.2 | async-start | bytes 4194304 | tf_op jit(solution)/shard_map/all_to_all | solution.py:244
  179.0 1.3 copy-start
  180.3 124.7 %all-to-all-start.1 = ((bf16[8,2,128,512]{3,2,1,0:T(8,128)(2,1)}), bf16[8,2,128,512]{3,2,1,0:T(8,128)(2,1)S(1)}, u32[]{:S(2)}, u32[]{:S(2)}) async-start(bf16[8,2,128,512]{3,2,1,0:T(8,128)(2,1)} %collective-permute-done.126), calls=%async_computation.1 | async-start | bytes 4194304 | tf_op jit(solution)/shard_map/all_to_all | solution.py:244
  199.4 53.3 %collective-permute-start.124 = (bf16[2,2,512,512]{3,2,1,0:T(8,128)(2,1)S(1)}, bf16[2,2,512,512]{3,2,1,0:T(8,128)(2,1)S(1)}, u32[]{:S(2)}, u32[]{:S(2)}) collective-permute-start(bf16[2,2,512,512]{3,2,1,0:T(8,128)(2,1)S(1)} %param.40), channel_id=1, source_target_pairs={{6,5},{14,13},{22,21},{30,29},{38,37},{46,45},{54,53},{62,61},{70,... | collective-permute-start | bytes 6291464 | tf_op jit(solution)/shard_map/cond/branch_40_fun/ppermute | solution.py:211
  252.7 2.0 copy-start.42
  258.4 1.6 copy-start.1
  265.4 39.5 %collective-permute-start.82 = (bf16[2,512,512]{2,1,0:T(8,128)(2,1)S(1)}, bf16[2,512,512]{2,1,0:T(8,128)(2,1)}, u32[]{:S(2)}, u32[]{:S(2)}) collective-permute-start(bf16[2,512,512]{2,1,0:T(8,128)(2,1)S(1)} %param.124), channel_id=1, source_target_pairs={{6,5},{14,13},{22,21},{30,29},{38,37},{46,45},{54,53},{62,61},{70,... | collective-permute-start | bytes 3145736 | tf_op jit(solution)/shard_map/cond/branch_40_fun/ppermute | solution.py:211
  310.4 35.5 %collective-permute-start.40 = (bf16[2,512,512]{2,1,0:T(8,128)(2,1)S(1)}, bf16[2,512,512]{2,1,0:T(8,128)(2,1)}, u32[]{:S(2)}, u32[]{:S(2)}) collective-permute-start(bf16[2,512,512]{2,1,0:T(8,128)(2,1)S(1)} %param.82), channel_id=1, source_target_pairs={{6,5},{14,13},{22,21},{30,29},{38,37},{46,45},{54,53},{62,61},{70,... | collective-permute-start | bytes 3145736 | tf_op jit(solution)/shard_map/cond/branch_40_fun/ppermute | solution.py:211
